TPU v7x, 512 devices: a whole 4x8x8 slice. The times are simulated.
512 devices in a mesh: row: 16 (over y_hi, x), pair: 32 (over y_lo, z, core).
Axes of the slice: x: 4, y: 8 (y_hi: 4, y_lo: 2; y = y_hi * 2 + y_lo), z: 8, core: 2. Of those that a mesh axis runs over, the one named last changes fastest.
Arguments:
- embedding: float32 [32768, 8192], P(('row', 'pair')), may hold values from -54 to 54
- pairing: int32 [64], replicated, may hold values from 0 to 63, each once
Outputs:
- rotated: float32 [32768, 8192], P('row', 'pair')
Inputs may be any that keep to these rules, and one draw needn't show every extreme that they name: `pairing`: each column block index from 0 to 63 appears exactly once.
All inputs are finite; a program needn't handle non-finite values.
Results may differ from a plain program's by a relative error of at most 0.0003.
Values sent between devices are 32-bit elements; how exact they have to be, the bound alone decides.
A program may use at most 64 MiB of HBM per device.

v0:
```python
import jax
import jax.numpy as jnp
from jax import lax
from jax.sharding import PartitionSpec as P

ROUNDS = 3
SWEEPS = 2


def gathered_total(array, axis):
    return lax.all_gather(array, axis).sum(0)


def shifted(block, axis, distance):
    devices = range(lax.axis_size(axis))
    route = [(i - distance, i) for i in devices if i - distance in devices]
    return lax.ppermute(block, axis, route)


def sent_to_all(array, axis):
    devices = lax.axis_size(axis)
    return lax.all_to_all(
        jnp.broadcast_to(array[None], (devices, *array.shape)), axis, 0, 0, tiled=True
    )


def taken_together(array, axis):
    return sent_to_all(array, axis).sum(axis=0)


def make_rotation(gram_mat, total_rows):
    width = gram_mat.shape[0]
    identity = jnp.eye(width, dtype=jnp.float32)
    current = gram_mat
    accumulated = identity
    for sweep in range(SWEEPS):
        scaled = current / total_rows
        level = jnp.diagonal(scaled) + 1e-06
        spread = level[None, :] - level[:, None]
        generator = scaled * spread / (spread * spread + 0.25 * level[:, None] * level[None, :])
        metric = identity - jnp.dot(generator, generator, precision=lax.Precision.HIGHEST)
        factor = jnp.linalg.cholesky(metric)
        turned_t = lax.linalg.triangular_solve(
            factor, identity - generator, left_side=True, lower=True
        )
        step_rot = turned_t.T
        if sweep == 0:
            accumulated = step_rot
        else:
            accumulated = jnp.dot(accumulated, step_rot, precision=lax.Precision.HIGHEST)
        if sweep + 1 < SWEEPS:
            half = jnp.dot(current, step_rot, precision=lax.Precision.HIGHEST)
            current = jnp.dot(step_rot.T, half, precision=lax.Precision.HIGHEST)
    return accumulated


def inner_rows(left_side, right_side):
    return lax.dot_general(
        left_side,
        right_side,
        (((0,), (0,)), ((), ())),
        precision=lax.Precision.HIGHEST,
        preferred_element_type=jnp.float32,
    )


def full_gram(upper_block, lower_block):
    pair_cols = jnp.concatenate([upper_block, lower_block], axis=1)
    return gathered_total(inner_rows(pair_cols, pair_cols), "row")


def move_blocks(upper_load, lower_load, position, last_index):
    sent_on = jnp.where(position == 0, lower_load, upper_load)
    came_on = shifted(sent_on, "pair", 1)
    came_back = shifted(lower_load, "pair", -1)
    new_upper = jnp.where(position == 0, upper_load, came_on)
    new_lower = jnp.where(position == last_index, upper_load, came_back)
    return (new_upper, new_lower)


def body(embedding, pairing):
    sub_rows, columns = embedding.shape
    slots = pairing.shape[0]
    block = columns // slots
    ordered = jnp.take(embedding.reshape(sub_rows, slots, block), pairing, axis=1).reshape(
        sub_rows, columns
    )
    local = lax.all_to_all(ordered, "pair", split_axis=1, concat_axis=0, tiled=True)
    rows_here = local.shape[0]
    total_rows = rows_here * lax.axis_size("row")
    position = lax.axis_index("pair")
    last_index = lax.axis_size("pair") - 1
    upper_block = local[:, :block]
    lower_block = local[:, block:]
    gram_mat = full_gram(upper_block, lower_block)
    for round_num in range(ROUNDS):
        rotation = make_rotation(gram_mat, total_rows)
        pair_cols = jnp.concatenate([upper_block, lower_block], axis=1)
        turned = jnp.dot(
            pair_cols, rotation, precision=lax.Precision.HIGHEST, preferred_element_type=jnp.float32
        )
        upper_block = turned[:, :block]
        lower_block = turned[:, block:]
        if round_num + 1 < ROUNDS:
            product = jnp.dot(
                gram_mat,
                rotation,
                precision=lax.Precision.HIGHEST,
                preferred_element_type=jnp.float32,
            )
            upper_gram = inner_rows(rotation[:, :block], product[:, :block])
            lower_gram = inner_rows(rotation[:, block:], product[:, block:])
            upper_load = jnp.concatenate([upper_block, upper_gram], axis=0)
            lower_load = jnp.concatenate([lower_block, lower_gram], axis=0)
            upper_load, lower_load = move_blocks(upper_load, lower_load, position, last_index)
            upper_block = upper_load[:rows_here]
            upper_gram = upper_load[rows_here:]
            lower_block = lower_load[:rows_here]
            lower_gram = lower_load[rows_here:]
            cross = taken_together(inner_rows(upper_block, lower_block), "row")
            gram_mat = jnp.concatenate(
                [
                    jnp.concatenate([upper_gram, cross], axis=1),
                    jnp.concatenate([cross.T, lower_gram], axis=1),
                ],
                axis=0,
            )
        else:
            upper_block, lower_block = move_blocks(upper_block, lower_block, position, last_index)
    return jnp.concatenate([upper_block, lower_block], axis=1)


def solution(mesh):
    in_specs = (P(("row", "pair"), None), P())
    out_specs = P("row", "pair")
    return jax.shard_map(body, mesh=mesh, in_specs=in_specs, out_specs=out_specs, check_vma=False)
```

profile of v0, /device:TPU:193, one launch (start us, length us, event | category | flops | bytes accessed | tf_op | source)
XLA Modules:
  0.0 728.0 jit_solution(877165816631199930)
XLA Ops:
  18.1 57.4 %all_to_all.26 = f32[64,32,256]{2,0,1:T(8,128)S(1)} all-to-all(f32[64,32,256]{2,0,1:T(8,128)S(1)} %copy_select_fusion), channel_id=1, replica_groups=mesh['row'=16,'pair'=32] {'pair'}, dimensions={1} | all-to-all | bytes 4194304 | tf_op jit(solution)/shard_map/all_to_all | solution.py:88
  79.9 76.8 %all-gather.3.cloned.1.call-done = f32[4096,256]{1,0:T(8,128)} async-done(((f32[256,256]{1,0:T(8,128)}), f32[4096,256]{1,0:T(8,128)}) %all-gather.3.cloned.1.call-update) | async-done | bytes 4194320 | tf_op jit(solution)/shard_map/all_gather | solution.py:11
  162.7 11.7 %cholesky.298 = f32[128,128]{1,0:T(8,128)S(1)} custom-call(f32[128,128]{1,0:T(8,128)S(1)} %cholesky.498), custom_call_target="Cholesky" | custom-call | tf_op jit(solution)/shard_map/jit(cholesky)/cholesky | solution.py:42
  174.5 9.8 %custom-call.33 = f32[1,128,128]{1,2,0:T(8,128)S(1)} custom-call(f32[1,128,128]{2,1,0:T(8,128)S(1)} %get-tuple-element.150), custom_call_target="InvertDiagBlocksLowerTriangular" | custom-call | tf_op jit(solution)/shard_map/jit(cholesky)/cholesky | solution.py:42
  184.8 11.7 %cholesky.315 = f32[128,128]{1,0:T(8,128)S(1)} custom-call(f32[128,128]{1,0:T(8,128)S(1)} %convolution_subtract_fusion.11), custom_call_target="Cholesky" | custom-call | tf_op jit(solution)/shard_map/jit(cholesky)/cholesky | solution.py:42
  202.9 19.9 %custom-call.34 = f32[2,128,128]{1,2,0:T(8,128)S(1)} custom-call(f32[2,128,128]{2,1,0:T(8,128)S(1)} %get-tuple-element.45), custom_call_target="InvertDiagBlocksLowerTriangular" | custom-call | tf_op jit(solution)/shard_map/triangular_solve/custom-call.0 | solution.py:43
  228.8 11.7 %cholesky.332 = f32[128,128]{1,0:T(8,128)S(1)} custom-call(f32[128,128]{1,0:T(8,128)S(1)} %cholesky.501), custom_call_target="Cholesky" | custom-call | tf_op jit(solution)/shard_map/jit(cholesky)/cholesky | solution.py:42
  240.6 9.8 %custom-call.35 = f32[1,128,128]{1,2,0:T(8,128)S(1)} custom-call(f32[1,128,128]{2,1,0:T(8,128)S(1)} %get-tuple-element.146), custom_call_target="InvertDiagBlocksLowerTriangular" | custom-call | tf_op jit(solution)/shard_map/jit(cholesky)/cholesky | solution.py:42
  252.6 11.7 %cholesky.349 = f32[128,128]{1,0:T(8,128)S(1)} custom-call(f32[128,128]{1,0:T(8,128)S(1)} %convolution_subtract_fusion.10), custom_call_target="Cholesky" | custom-call | tf_op jit(solution)/shard_map/jit(cholesky)/cholesky | solution.py:42
  271.2 20.1 %custom-call.36 = f32[2,128,128]{1,2,0:T(8,128)S(1)} custom-call(f32[2,128,128]{2,1,0:T(8,128)S(1)} %get-tuple-element.46), custom_call_target="InvertDiagBlocksLowerTriangular" | custom-call | tf_op jit(solution)/shard_map/triangular_solve/custom-call.0 | solution.py:43
  304.6 10.8 %collective-permute-done = f32[2176,128]{0,1:T(8,128)S(1)} collective-permute-done((f32[2176,128]{0,1:T(8,128)}, f32[2176,128]{0,1:T(8,128)S(1)}, u32[]{:S(2)}, u32[]{:S(2)}) %collective-permute-start) | collective-permute-done | bytes 1114144 | tf_op jit(solution)/shard_map/ppermute | solution.py:17
  324.7 10.9 %all-to-all-start.1 = ((f32[16,128,128]{2,1,0:T(8,128)}), f32[16,128,128]{2,1,0:T(8,128)}, u32[]{:S(2)}, u32[]{:S(2)}) async-start(f32[16,128,128]{2,1,0:T(8,128)} %broadcast_in_dim.43), calls=%async_computation.1 | async-start | bytes 2097152 | tf_op jit(solution)/shard_map/all_to_all | solution.py:22
  335.9 26.4 %all-to-all-done.1 = f32[16,128,128]{2,1,0:T(8,128)} async-done(((f32[16,128,128]{2,1,0:T(8,128)}), f32[16,128,128]{2,1,0:T(8,128)}, u32[]{:S(2)}, u32[]{:S(2)}) %all-to-all-start.1) | async-done | bytes 1048608 | tf_op jit(solution)/shard_map/all_to_all | solution.py:22
  367.0 11.7 %cholesky.366 = f32[128,128]{1,0:T(8,128)S(1)} custom-call(f32[128,128]{1,0:T(8,128)S(1)} %cholesky.504), custom_call_target="Cholesky" | custom-call | tf_op jit(solution)/shard_map/jit(cholesky)/cholesky | solution.py:42
  378.8 9.8 %custom-call.37 = f32[1,128,128]{1,2,0:T(8,128)S(1)} custom-call(f32[1,128,128]{2,1,0:T(8,128)S(1)} %get-tuple-element.142), custom_call_target="InvertDiagBlocksLowerTriangular" | custom-call | tf_op jit(solution)/shard_map/jit(cholesky)/cholesky | solution.py:42
  389.1 11.7 %cholesky.383 = f32[128,128]{1,0:T(8,128)S(1)} custom-call(f32[128,128]{1,0:T(8,128)S(1)} %convolution_subtract_fusion.9), custom_call_target="Cholesky" | custom-call | tf_op jit(solution)/shard_map/jit(cholesky)/cholesky | solution.py:42
  407.7 20.1 %custom-call.38 = f32[2,128,128]{1,2,0:T(8,128)S(1)} custom-call(f32[2,128,128]{2,1,0:T(8,128)S(1)} %get-tuple-element.47), custom_call_target="InvertDiagBlocksLowerTriangular" | custom-call | tf_op jit(solution)/shard_map/triangular_solve/custom-call.0 | solution.py:43
  434.0 11.7 %cholesky.400 = f32[128,128]{1,0:T(8,128)S(1)} custom-call(f32[128,128]{1,0:T(8,128)S(1)} %cholesky.507), custom_call_target="Cholesky" | custom-call | tf_op jit(solution)/shard_map/jit(cholesky)/cholesky | solution.py:42
  445.8 9.8 %custom-call.39 = f32[1,128,128]{1,2,0:T(8,128)S(1)} custom-call(f32[1,128,128]{2,1,0:T(8,128)S(1)} %get-tuple-element.138), custom_call_target="InvertDiagBlocksLowerTriangular" | custom-call | tf_op jit(solution)/shard_map/jit(cholesky)/cholesky | solution.py:42
  457.7 11.7 %cholesky.417 = f32[128,128]{1,0:T(8,128)S(1)} custom-call(f32[128,128]{1,0:T(8,128)S(1)} %convolution_subtract_fusion.8), custom_call_target="Cholesky" | custom-call | tf_op jit(solution)/shard_map/jit(cholesky)/cholesky | solution.py:42
  476.4 19.9 %custom-call.40 = f32[2,128,128]{1,2,0:T(8,128)S(1)} custom-call(f32[2,128,128]{2,1,0:T(8,128)S(1)} %get-tuple-element.48), custom_call_target="InvertDiagBlocksLowerTriangular" | custom-call | tf_op jit(solution)/shard_map/triangular_solve/custom-call.0 | solution.py:43
  508.6 10.5 %collective-permute-done.2 = f32[2176,128]{0,1:T(8,128)S(1)} collective-permute-done((f32[2176,128]{0,1:T(8,128)S(1)}, f32[2176,128]{0,1:T(8,128)S(1)}, u32[]{:S(2)}, u32[]{:S(2)}) %collective-permute-start.2) | collective-permute-done | bytes 1114144 | tf_op jit(solution)/shard_map/ppermute | solution.py:17
  532.1 23.4 %all-to-all-done.2 = f32[16,128,128]{2,1,0:T(8,128)} async-done(((f32[16,128,128]{2,1,0:T(8,128)}), f32[16,128,128]{2,1,0:T(8,128)}, u32[]{:S(2)}, u32[]{:S(2)}) %all-to-all-start.2) | async-done | bytes 1048608 | tf_op jit(solution)/shard_map/all_to_all | solution.py:22
  560.2 11.7 %cholesky.434 = f32[128,128]{1,0:T(8,128)S(1)} custom-call(f32[128,128]{1,0:T(8,128)S(1)} %cholesky.510), custom_call_target="Cholesky" | custom-call | tf_op jit(solution)/shard_map/jit(cholesky)/cholesky | solution.py:42
  571.9 9.8 %custom-call.41 = f32[1,128,128]{1,2,0:T(8,128)S(1)} custom-call(f32[1,128,128]{2,1,0:T(8,128)S(1)} %get-tuple-element.134), custom_call_target="InvertDiagBlocksLowerTriangular" | custom-call | tf_op jit(solution)/shard_map/jit(cholesky)/cholesky | solution.py:42
  582.2 11.7 %cholesky.451 = f32[128,128]{1,0:T(8,128)S(1)} custom-call(f32[128,128]{1,0:T(8,128)S(1)} %convolution_subtract_fusion.7), custom_call_target="Cholesky" | custom-call | tf_op jit(solution)/shard_map/jit(cholesky)/cholesky | solution.py:42
  600.8 19.8 %custom-call.42 = f32[2,128,128]{1,2,0:T(8,128)S(1)} custom-call(f32[2,128,128]{2,1,0:T(8,128)S(1)} %get-tuple-element.49), custom_call_target="InvertDiagBlocksLowerTriangular" | custom-call | tf_op jit(solution)/shard_map/triangular_solve/custom-call.0 | solution.py:43
  626.2 11.7 %cholesky.468 = f32[128,128]{1,0:T(8,128)S(1)} custom-call(f32[128,128]{1,0:T(8,128)S(1)} %cholesky.513), custom_call_target="Cholesky" | custom-call | tf_op jit(solution)/shard_map/jit(cholesky)/cholesky | solution.py:42
  638.0 9.8 %custom-call.43 = f32[1,128,128]{1,2,0:T(8,128)S(1)} custom-call(f32[1,128,128]{2,1,0:T(8,128)S(1)} %get-tuple-element.130), custom_call_target="InvertDiagBlocksLowerTriangular" | custom-call | tf_op jit(solution)/shard_map/jit(cholesky)/cholesky | solution.py:42
  648.3 11.7 %cholesky.485 = f32[128,128]{1,0:T(8,128)S(1)} custom-call(f32[128,128]{1,0:T(8,128)S(1)} %convolution_subtract_fusion.6), custom_call_target="Cholesky" | custom-call | tf_op jit(solution)/shard_map/jit(cholesky)/cholesky | solution.py:42
  666.9 19.9 %custom-call.44 = f32[2,128,128]{1,2,0:T(8,128)S(1)} custom-call(f32[2,128,128]{2,1,0:T(8,128)S(1)} %get-tuple-element.50), custom_call_target="InvertDiagBlocksLowerTriangular" | custom-call | tf_op jit(solution)/shard_map/triangular_solve/custom-call.0 | solution.py:43
  700.9 9.8 %collective-permute-done.4 = f32[2048,128]{0,1:T(8,128)S(1)} collective-permute-done((f32[2048,128]{0,1:T(8,128)S(1)}, f32[2048,128]{0,1:T(8,128)S(1)}, u32[]{:S(2)}, u32[]{:S(2)}) %collective-permute-start.4) | collective-permute-done | bytes 1048608 | tf_op jit(solution)/shard_map/ppermute | solution.py:17
  (241 shorter events, 184.4 us)
Async XLA Ops:
  6.5 1.6 copy-start
  6.5 150.1 %all-gather.3.cloned.1.call-start = ((), (), s32[]{:S(2)}) async-start(), calls=%async_computation.3 | async-start | bytes 4456448 | tf_op jit(solution)/shard_map/all_gather | solution.py:11
  228.1 0.7 copy-start.3
  297.5 18.0 %collective-permute-start = (f32[2176,128]{0,1:T(8,128)}, f32[2176,128]{0,1:T(8,128)S(1)}, u32[]{:S(2)}, u32[]{:S(2)}) collective-permute-start(f32[2176,128]{0,1:T(8,128)} %get-tuple-element.125), channel_id=1, source_target_pairs={{0,1},{1,2},{2,3},{3,4},{4,5},{5,6},{6,7},{7,8},{8,9},{9,10},{10,1... | collective-permute-start | bytes 3342344 | tf_op jit(solution)/shard_map/ppermute | solution.py:17
  302.7 18.1 %collective-permute-start.1 = (f32[2176,128]{0,1:T(8,128)S(1)}, f32[2176,128]{0,1:T(8,128)}, u32[]{:S(2)}, u32[]{:S(2)}) collective-permute-start(f32[2176,128]{0,1:T(8,128)S(1)} %get-tuple-element.126), channel_id=1, source_target_pairs={{1,0},{2,1},{3,2},{4,3},{5,4},{6,5},{7,6},{8,7},{9,8},{10,9},{11,1... | collective-permute-start | bytes 3342344 | tf_op jit(solution)/shard_map/ppermute | solution.py:17
  315.4 1.0 copy-start.2
  324.7 37.5 %all-to-all-start.1 = ((f32[16,128,128]{2,1,0:T(8,128)}), f32[16,128,128]{2,1,0:T(8,128)}, u32[]{:S(2)}, u32[]{:S(2)}) async-start(f32[16,128,128]{2,1,0:T(8,128)} %broadcast_in_dim.43), calls=%async_computation.1 | async-start | bytes 2097152 | tf_op jit(solution)/shard_map/all_to_all | solution.py:22
  433.3 0.7 copy-start.4
  501.7 17.4 %collective-permute-start.2 = (f32[2176,128]{0,1:T(8,128)S(1)}, f32[2176,128]{0,1:T(8,128)S(1)}, u32[]{:S(2)}, u32[]{:S(2)}) collective-permute-start(f32[2176,128]{0,1:T(8,128)S(1)} %get-tuple-element.121), channel_id=1, source_target_pairs={{0,1},{1,2},{2,3},{3,4},{4,5},{5,6},{6,7},{7,8},{8,9},{9,10},{10,1... | collective-permute-start | bytes 3342344 | tf_op jit(solution)/shard_map/ppermute | solution.py:17
  506.6 18.0 %collective-permute-start.3 = (f32[2176,128]{0,1:T(8,128)S(1)}, f32[2176,128]{0,1:T(8,128)S(1)}, u32[]{:S(2)}, u32[]{:S(2)}) collective-permute-start(f32[2176,128]{0,1:T(8,128)S(1)} %get-tuple-element.122), channel_id=1, source_target_pairs={{1,0},{2,1},{3,2},{4,3},{5,4},{6,5},{7,6},{8,7},{9,8},{10,9},{11,1... | collective-permute-start | bytes 3342344 | tf_op jit(solution)/shard_map/ppermute | solution.py:17
  526.9 28.5 %all-to-all-start.2 = ((f32[16,128,128]{2,1,0:T(8,128)}), f32[16,128,128]{2,1,0:T(8,128)}, u32[]{:S(2)}, u32[]{:S(2)}) async-start(f32[16,128,128]{2,1,0:T(8,128)} %broadcast_in_dim.76), calls=%async_computation.2 | async-start | bytes 2097152 | tf_op jit(solution)/shard_map/all_to_all | solution.py:22
  690.7 19.9 %collective-permute-start.4 = (f32[2048,128]{0,1:T(8,128)S(1)}, f32[2048,128]{0,1:T(8,128)S(1)}, u32[]{:S(2)}, u32[]{:S(2)}) collective-permute-start(f32[2048,128]{0,1:T(8,128)S(1)} %get-tuple-element.113), channel_id=1, source_target_pairs={{0,1},{1,2},{2,3},{3,4},{4,5},{5,6},{6,7},{7,8},{8,9},{9,10},{10,1... | collective-permute-start | bytes 3145736 | tf_op jit(solution)/shard_map/ppermute | solution.py:17
  698.9 17.3 %collective-permute-start.5 = (f32[2048,128]{0,1:T(8,128)S(1)}, f32[2048,128]{0,1:T(8,128)S(1)}, u32[]{:S(2)}, u32[]{:S(2)}) collective-permute-start(f32[2048,128]{0,1:T(8,128)S(1)} %get-tuple-element.114), channel_id=1, source_target_pairs={{1,0},{2,1},{3,2},{4,3},{5,4},{6,5},{7,6},{8,7},{9,8},{10,9},{11,1... | collective-permute-start | bytes 3145736 | tf_op jit(solution)/shard_map/ppermute | solution.py:17
  716.5 4.4 copy-start.1
Sparse Core Ops, SparseCore 0:
  79.9 76.6 all-gather.2
where the time goes:
time: 735 us; the launch traced here: 728 us
  other arithmetic  341 us (46%)
  waiting for transfers between devices  173 us (24%)
  blocking collectives  57.4 us (8%)
  local copies, waits for them, and re-layouts  56.9 us (8%)
  starting transfers between devices  39.9 us (5%)
  matrix products  35.8 us (5%)
  between operations  22.9 us (3%)
    another operation x41, other arithmetic, make_rotation(): factor = jnp.linalg.cholesky(metric)  207 us
    another operation x13, other arithmetic, make_rotation(): lax.linalg.triangular_solve(factor, identity - generator, left_side=True,...  120 us
    all_gather x1, waiting for transfers between devices, gathered_total(): return lax.all_gather(array, axis).sum(0)  76.8 us
    all_to_all x1, blocking collectives, body(): lax.all_to_all(ordered, 'pair', split_axis=1, concat_axis=0, tiled=True)  57.4 us
    all_to_all x2, waiting for transfers between devices, sent_to_all(): lax.all_to_all(jnp.broadcast_to(array[None], (devices, *array.shape)), ax...  49.7 us
    ppermute x6, waiting for transfers between devices, shifted(): return lax.ppermute(block, axis, route)  46.7 us
    another operation x43, local copies, waits for them, and re-layouts, make_rotation(): lax.linalg.triangular_solve(factor, identity - generator, left_side=True,...  24.5 us
    ppermute x6, starting transfers between devices, shifted(): return lax.ppermute(block, axis, route)  24.1 us
  transfers between devices with their start and end apart: 9, of which 9 were waited for; matrix products, arithmetic and copies ran while one was open for 0% of the time, Pallas kernels for 0%

commit v1 on v0

--- a/solution.py
+++ b/solution.py
@@ -1,10 +1,143 @@
+import functools
+
 import jax
 import jax.numpy as jnp
 from jax import lax
+from jax.experimental import pallas as pl
+from jax.experimental.pallas import tpu as pltpu
 from jax.sharding import PartitionSpec as P
 
 ROUNDS = 3
 SWEEPS = 2
+F32 = jnp.float32
+BF16 = jnp.bfloat16
+
+
+def halves(a):
+    high = a.astype(BF16)
+    return high, (a - high.astype(F32)).astype(BF16)
+
+
+def product(a, b, dims=((1,), (0,))):
+    def one(x, y):
+        return lax.dot_general(x, y, (dims, ((), ())), preferred_element_type=F32)
+
+    a_high, a_low = a
+    b_high, b_low = b
+    return one(a_high, b_high) + (one(a_high, b_low) + one(a_low, b_high))
+
+
+def rotation_kernel(total_rows, gram_ref, rotation_ref, upper_ref, lower_ref, current, basis, level, strict):
+    width = gram_ref.shape[0]
+    block = width // 2
+    rows = lax.broadcasted_iota(jnp.int32, (width, width), 0)
+    cols = lax.broadcasted_iota(jnp.int32, (width, width), 1)
+    eye = rows == cols
+    above = rows < cols
+
+    def diag_row(a):
+        return jnp.sum(jnp.where(eye, a, 0.0), axis=0, keepdims=True)
+
+    def diag_col(a):
+        return jnp.sum(jnp.where(eye, a, 0.0), axis=1, keepdims=True)
+
+    current[...] = gram_ref[...]
+    for sweep in range(SWEEPS):
+        scaled = current[...] * (1.0 / total_rows)
+        level_row = diag_row(scaled) + 1e-06
+        level_col = diag_col(scaled) + 1e-06
+        spread = level_row - level_col
+        generator = scaled * spread / (spread * spread + 0.25 * level_col * level_row)
+        parts = halves(generator)
+        square = product(parts, parts)
+        basis[...] = jnp.where(eye, 1.0, 0.0) + generator
+        level[...] = 1.0 - diag_col(square)
+        strict[...] = jnp.where(above, -square, 0.0)
+        size = jnp.sum(square * square * jnp.where(above, 1.0, 0.0))
+
+        @pl.when(size > 0.0625)
+        def _():
+            exact = jnp.dot(generator, generator, precision=lax.Precision.HIGHEST, preferred_element_type=F32)
+            current_metric = jnp.where(eye, 1.0, 0.0) - exact
+            strict[...] = 0.5 * (current_metric + current_metric.T)
+
+            def step(k, _):
+                pivot_row = strict[pl.ds(k, 1), :]
+                lane = lax.broadcasted_iota(jnp.int32, (1, width), 1)
+                pivot = jnp.sum(jnp.where(lane == k, pivot_row, 0.0), axis=1, keepdims=True)
+                after = jnp.where(lane > k, pivot_row / pivot, 0.0)
+                metric = strict[...]
+                pivot_col = jnp.sum(jnp.where(cols == k, metric, 0.0), axis=1, keepdims=True)
+                strict[...] = metric - pivot_col * after
+                turned = basis[...]
+                basis_col = jnp.sum(jnp.where(cols == k, turned, 0.0), axis=1, keepdims=True)
+                basis[...] = turned - basis_col * after
+                return 0
+
+            lax.fori_loop(0, width, step, 0)
+            level[...] = diag_col(strict[...])
+            strict[...] = jnp.zeros_like(strict)
+
+        def eliminate(state):
+            _, count = state
+            upper = strict[...]
+            scale = level[...]
+            ratio = upper / scale
+            ratio_parts = halves(ratio)
+            turned = basis[...]
+            basis[...] = turned - product(halves(turned), ratio_parts)
+            size_now = jnp.sum(upper * upper)
+
+            @pl.when(size_now > 1e-06)
+            def _():
+                second = product(halves(upper), ratio_parts)
+                mixed = product(halves(ratio.T), halves(0.5 * upper - second))
+                level[...] = scale - 2.0 * diag_col(mixed)
+                strict[...] = jnp.where(above, -(second + mixed + mixed.T), 0.0)
+
+            return size_now, count + 1
+
+        lax.while_loop(
+            lambda state: jnp.logical_and(state[0] > 1e-06, state[1] < width),
+            eliminate,
+            (jnp.float32(1.0), jnp.int32(0)),
+        )
+        level_out = jnp.sum(jnp.where(eye, jnp.broadcast_to(level[...], (width, width)), 0.0), axis=0, keepdims=True)
+        step_rot = basis[...] * lax.rsqrt(level_out)
+        step_parts = halves(step_rot)
+        half = product(halves(current[...]), step_parts)
+        if sweep == 0:
+            rotation_ref[...] = step_rot
+        else:
+            rotation_ref[...] = product(halves(rotation_ref[...]), step_parts)
+        if sweep + 1 < SWEEPS:
+            current[...] = product(halves(step_rot.T), halves(half))
+        else:
+            turned_t = step_rot.T
+            upper_ref[...] = product(halves(turned_t[:block]), halves(half[:, :block]))
+            lower_ref[...] = product(halves(turned_t[block:]), halves(half[:, block:]))
+
+
+def make_rotation(gram, total_rows):
+    width = gram.shape[0]
+    block = width // 2
+    return pl.pallas_call(
+        functools.partial(rotation_kernel, total_rows),
+        out_shape=(
+            jax.ShapeDtypeStruct((width, width), F32),
+            jax.ShapeDtypeStruct((block, block), F32),
+            jax.ShapeDtypeStruct((block, block), F32),
+        ),
+        in_specs=[pl.BlockSpec(memory_space=pltpu.VMEM)],
+        out_specs=(pl.BlockSpec(memory_space=pltpu.VMEM),) * 3,
+        scratch_shapes=[
+            pltpu.VMEM((width, width), F32),
+            pltpu.VMEM((width, width), F32),
+            pltpu.VMEM((width, 1), F32),
+            pltpu.VMEM((width, width), F32),
+        ],
+        name="rotation",
+    )(gram)
 
 
 def gathered_total(array, axis):
@@ -26,32 +159,6 @@
 
 def taken_together(array, axis):
     return sent_to_all(array, axis).sum(axis=0)
-
-
-def make_rotation(gram_mat, total_rows):
-    width = gram_mat.shape[0]
-    identity = jnp.eye(width, dtype=jnp.float32)
-    current = gram_mat
-    accumulated = identity
-    for sweep in range(SWEEPS):
-        scaled = current / total_rows
-        level = jnp.diagonal(scaled) + 1e-06
-        spread = level[None, :] - level[:, None]
-        generator = scaled * spread / (spread * spread + 0.25 * level[:, None] * level[None, :])
-        metric = identity - jnp.dot(generator, generator, precision=lax.Precision.HIGHEST)
-        factor = jnp.linalg.cholesky(metric)
-        turned_t = lax.linalg.triangular_solve(
-            factor, identity - generator, left_side=True, lower=True
-        )
-        step_rot = turned_t.T
-        if sweep == 0:
-            accumulated = step_rot
-        else:
-            accumulated = jnp.dot(accumulated, step_rot, precision=lax.Precision.HIGHEST)
-        if sweep + 1 < SWEEPS:
-            half = jnp.dot(current, step_rot, precision=lax.Precision.HIGHEST)
-            current = jnp.dot(step_rot.T, half, precision=lax.Precision.HIGHEST)
-    return accumulated
 
 
 def inner_rows(left_side, right_side):
@@ -94,7 +201,7 @@
     lower_block = local[:, block:]
     gram_mat = full_gram(upper_block, lower_block)
     for round_num in range(ROUNDS):
-        rotation = make_rotation(gram_mat, total_rows)
+        rotation, upper_gram, lower_gram = make_rotation(gram_mat, total_rows)
         pair_cols = jnp.concatenate([upper_block, lower_block], axis=1)
         turned = jnp.dot(
             pair_cols, rotation, precision=lax.Precision.HIGHEST, preferred_element_type=jnp.float32
@@ -102,14 +209,6 @@
         upper_block = turned[:, :block]
         lower_block = turned[:, block:]
         if round_num + 1 < ROUNDS:
-            product = jnp.dot(
-                gram_mat,
-                rotation,
-                precision=lax.Precision.HIGHEST,
-                preferred_element_type=jnp.float32,
-            )
-            upper_gram = inner_rows(rotation[:, :block], product[:, :block])
-            lower_gram = inner_rows(rotation[:, block:], product[:, block:])
             upper_load = jnp.concatenate([upper_block, upper_gram], axis=0)
             lower_load = jnp.concatenate([lower_block, lower_gram], axis=0)
             upper_load, lower_load = move_blocks(upper_load, lower_load, position, last_index)

time: 735 us -> 590 us (0.80)
  the two profiles are of different devices: /device:TPU:193 before, /device:TPU:207 now
where the time goes in v1:
time: 590 us; the launch traced here: 586 us
  Pallas kernels  252 us (43%)
  waiting for transfers between devices  162 us (27%)
  blocking collectives  56.6 us (10%)
  starting transfers between devices  34.3 us (6%)
  local copies, waits for them, and re-layouts  32.2 us (5%)
  matrix products  18 us (3%)
  other arithmetic  17.5 us (3%)
  between operations  13.7 us (2%)
    pallas_call x3, Pallas kernels, make_rotation(): pl.pallas_call(functools.partial(rotation_kernel, total_rows), out_shape=...  252 us
    all_gather x1, waiting for transfers between devices, gathered_total(): return lax.all_gather(array, axis).sum(0)  81.9 us
    all_to_all x1, blocking collectives, body(): lax.all_to_all(ordered, 'pair', split_axis=1, concat_axis=0, tiled=True)  56.6 us
    ppermute x6, waiting for transfers between devices, shifted(): return lax.ppermute(block, axis, route)  46.4 us
    all_to_all x2, waiting for transfers between devices, sent_to_all(): lax.all_to_all(jnp.broadcast_to(array[None], (devices, *array.shape)), ax...  33.4 us
    ppermute x6, starting transfers between devices, shifted(): return lax.ppermute(block, axis, route)  18 us
    all_to_all x2, starting transfers between devices, sent_to_all(): lax.all_to_all(jnp.broadcast_to(array[None], (devices, *array.shape)), ax...  16.3 us
  transfers between devices with their start and end apart: 9, of which 9 were waited for; matrix products, arithmetic and copies ran while one was open for 1% of the time, Pallas kernels for 0%

profile of v1, /device:TPU:207, one launch (start us, length us, event | category | flops | bytes accessed | tf_op | source)
XLA Modules:
  0.0 586.2 jit_solution(5221850709635675968)
XLA Ops:
  9.7 3.6 gather_fusion
  13.3 4.1 copy.18
  17.5 2.9 gather.7
  20.6 2.9 copy_select_fusion
  23.5 56.6 %all_to_all.26 = f32[64,32,256]{2,0,1:T(8,128)S(1)} all-to-all(f32[64,32,256]{2,0,1:T(8,128)S(1)} %copy_select_fusion), channel_id=1, replica_groups=mesh['row'=16,'pair'=32] {'pair'}, dimensions={1} | all-to-all | bytes 4194304 | tf_op jit(solution)/shard_map/all_to_all | solution.py:195
  81.5 4.4 fusion.10
  85.9 81.9 %all-gather.3.cloned.1.call-done = f32[4096,256]{1,0:T(8,128)} async-done(((f32[256,256]{1,0:T(8,128)}), f32[4096,256]{1,0:T(8,128)}) %all-gather.3.cloned.1.call-update) | async-done | bytes 4194320 | tf_op jit(solution)/shard_map/all_gather | solution.py:144
  167.8 3.2 reduce_sum.27.gram_ref
  171.0 84.0 %rotation.3 = (f32[256,256]{1,0:T(8,128)}, f32[128,128]{1,0:T(8,128)}, f32[128,128]{1,0:T(8,128)}) custom-call(f32[256,256]{1,0:T(8,128)} %reduce_sum.27.gram_ref), custom_call_target="tpu_custom_call" | custom-call | tf_op jit(solution)/shard_map/rotation/pallas_call | solution.py:124
  255.0 3.5 fusion.29
  260.9 5.0 collective-permute-start
  265.9 1.9 collective-permute-start.1
  267.8 10.8 %collective-permute-done = f32[2176,128]{1,0:T(8,128)S(1)} collective-permute-done((f32[2176,128]{1,0:T(8,128)}, f32[2176,128]{1,0:T(8,128)S(1)}, u32[]{:S(2)}, u32[]{:S(2)}) %collective-permute-start) | collective-permute-done | bytes 1114144 | tf_op jit(solution)/shard_map/ppermute | solution.py:150
  279.6 4.6 collective-permute-done.1
  284.2 2.1 fusion.17
  290.3 5.8 all-to-all-start.1
  296.9 2.3 slice.63
  300.3 15.5 %all-to-all-done.1 = f32[16,128,128]{2,1,0:T(8,128)} async-done(((f32[16,128,128]{2,1,0:T(8,128)}), f32[16,128,128]{2,1,0:T(8,128)}, u32[]{:S(2)}, u32[]{:S(2)}) %all-to-all-start.1) | async-done | bytes 1048608 | tf_op jit(solution)/shard_map/all_to_all | solution.py:155
  317.8 84.1 %rotation.4 = (f32[256,256]{1,0:T(8,128)}, f32[128,128]{1,0:T(8,128)}, f32[128,128]{1,0:T(8,128)}) custom-call(f32[256,256]{1,0:T(8,128)} %maximum_maximum_fusion.gram_ref), custom_call_target="tpu_custom_call" | custom-call | tf_op jit(solution)/shard_map/rotation/pallas_call | solution.py:124
  401.9 3.2 fusion
  406.1 4.8 collective-permute-start.2
  412.9 10.5 %collective-permute-done.2 = f32[2176,128]{1,0:T(8,128)S(1)} collective-permute-done((f32[2176,128]{1,0:T(8,128)S(1)}, f32[2176,128]{1,0:T(8,128)S(1)}, u32[]{:S(2)}, u32[]{:S(2)}) %collective-permute-start.2) | collective-permute-done | bytes 1114144 | tf_op jit(solution)/shard_map/ppermute | solution.py:150
  423.4 5.6 collective-permute-done.3
  433.1 10.5 %all-to-all-start.2 = ((f32[16,128,128]{2,1,0:T(8,128)}), f32[16,128,128]{2,1,0:T(8,128)}, u32[]{:S(2)}, u32[]{:S(2)}) async-start(f32[16,128,128]{2,1,0:T(8,128)} %broadcast_in_dim.37), calls=%async_computation.2 | async-start | bytes 2097152 | tf_op jit(solution)/shard_map/all_to_all | solution.py:155
  444.5 2.3 slice.69
  447.9 18.0 %all-to-all-done.2 = f32[16,128,128]{2,1,0:T(8,128)} async-done(((f32[16,128,128]{2,1,0:T(8,128)}), f32[16,128,128]{2,1,0:T(8,128)}, u32[]{:S(2)}, u32[]{:S(2)}) %all-to-all-start.2) | async-done | bytes 1048608 | tf_op jit(solution)/shard_map/all_to_all | solution.py:155
  467.9 84.1 %rotation.5 = (f32[256,256]{1,0:T(8,128)}, f32[128,128]{1,0:T(8,128)}, f32[128,128]{1,0:T(8,128)}) custom-call(f32[256,256]{1,0:T(8,128)} %maximum_maximum_fusion.1.gram_ref), custom_call_target="tpu_custom_call" | custom-call | tf_op jit(solution)/shard_map/rotation/pallas_call | solution.py:124
  552.0 3.3 fusion.4
  557.4 2.4 collective-permute-start.5
  559.9 9.3 %collective-permute-done.4 = f32[2048,128]{0,1:T(8,128)S(1)} collective-permute-done((f32[2048,128]{0,1:T(8,128)S(1)}, f32[2048,128]{0,1:T(8,128)S(1)}, u32[]{:S(2)}, u32[]{:S(2)}) %collective-permute-start.4) | collective-permute-done | bytes 1048608 | tf_op jit(solution)/shard_map/ppermute | solution.py:150
  569.2 5.6 collective-permute-done.5
  576.5 2.9 copy.22
  (59 shorter events, 30.9 us)
Async XLA Ops:
  6.5 1.6 copy-start
  6.5 161.2 %all-gather.3.cloned.1.call-start = ((), (), s32[]{:S(2)}) async-start(), calls=%async_computation.3 | async-start | bytes 4456448 | tf_op jit(solution)/shard_map/all_gather | solution.py:144
  80.2 1.3 copy-start.4
  258.5 0.8 copy-start.8
  258.5 0.9 copy-start.11
  258.7 2.2 copy-start.3
  260.9 17.7 %collective-permute-start = (f32[2176,128]{1,0:T(8,128)}, f32[2176,128]{1,0:T(8,128)S(1)}, u32[]{:S(2)}, u32[]{:S(2)}) collective-permute-start(f32[2176,128]{1,0:T(8,128)} %get-tuple-element.33), channel_id=1, source_target_pairs={{0,1},{1,2},{2,3},{3,4},{4,5},{5,6},{6,7},{7,8},{8,9},{9,10},{10,1... | collective-permute-start | bytes 3342344 | tf_op jit(solution)/shard_map/ppermute | solution.py:150
  265.9 18.3 %collective-permute-start.1 = (f32[2176,128]{1,0:T(8,128)}, f32[2176,128]{1,0:T(8,128)}, u32[]{:S(2)}, u32[]{:S(2)}) collective-permute-start(f32[2176,128]{1,0:T(8,128)} %get-tuple-element.34), channel_id=1, source_target_pairs={{1,0},{2,1},{3,2},{4,3},{5,4},{6,5},{7,6},{8,7},{9,8},{10,9},{11,1... | collective-permute-start | bytes 3342344 | tf_op jit(solution)/shard_map/ppermute | solution.py:150
  278.6 1.0 copy-start.7
  286.3 1.0 copy-start.1
  290.3 25.4 %all-to-all-start.1 = ((f32[16,128,128]{2,1,0:T(8,128)}), f32[16,128,128]{2,1,0:T(8,128)}, u32[]{:S(2)}, u32[]{:S(2)}) async-start(f32[16,128,128]{2,1,0:T(8,128)} %broadcast_in_dim.36), calls=%async_computation.1 | async-start | bytes 2097152 | tf_op jit(solution)/shard_map/all_to_all | solution.py:155
  300.3 101.6 %copy-start.6 = (f32[2048,128]{1,0:T(8,128)S(1)}, f32[2048,128]{1,0:T(8,128)}, u32[]{:S(2)}) copy-start(f32[2048,128]{1,0:T(8,128)} %slice.63) | copy-start | bytes 3145732
  405.1 0.8 copy-start.9
  405.1 0.9 copy-start.10
  406.1 17.3 %collective-permute-start.2 = (f32[2176,128]{1,0:T(8,128)S(1)}, f32[2176,128]{1,0:T(8,128)S(1)}, u32[]{:S(2)}, u32[]{:S(2)}) collective-permute-start(f32[2176,128]{1,0:T(8,128)S(1)} %get-tuple-element.29), channel_id=1, source_target_pairs={{0,1},{1,2},{2,3},{3,4},{4,5},{5,6},{6,7},{7,8},{8,9},{9,10},{10,1... | collective-permute-start | bytes 3342344 | tf_op jit(solution)/shard_map/ppermute | solution.py:150
  410.9 18.0 %collective-permute-start.3 = (f32[2176,128]{1,0:T(8,128)S(1)}, f32[2176,128]{1,0:T(8,128)S(1)}, u32[]{:S(2)}, u32[]{:S(2)}) collective-permute-start(f32[2176,128]{1,0:T(8,128)S(1)} %get-tuple-element.30), channel_id=1, source_target_pairs={{1,0},{2,1},{3,2},{4,3},{5,4},{6,5},{7,6},{8,7},{9,8},{10,9},{11,1... | collective-permute-start | bytes 3342344 | tf_op jit(solution)/shard_map/ppermute | solution.py:150
  429.2 1.0 copy-start.2
  433.1 32.7 %all-to-all-start.2 = ((f32[16,128,128]{2,1,0:T(8,128)}), f32[16,128,128]{2,1,0:T(8,128)}, u32[]{:S(2)}, u32[]{:S(2)}) async-start(f32[16,128,128]{2,1,0:T(8,128)} %broadcast_in_dim.37), calls=%async_computation.2 | async-start | bytes 2097152 | tf_op jit(solution)/shard_map/all_to_all | solution.py:155
  447.9 104.2 %copy-start.5 = (f32[2048,128]{1,0:T(8,128)S(1)}, f32[2048,128]{1,0:T(8,128)}, u32[]{:S(2)}) copy-start(f32[2048,128]{1,0:T(8,128)} %slice.69) | copy-start | bytes 3145732
  555.5 13.7 %collective-permute-start.4 = (f32[2048,128]{0,1:T(8,128)S(1)}, f32[2048,128]{0,1:T(8,128)S(1)}, u32[]{:S(2)}, u32[]{:S(2)}) collective-permute-start(f32[2048,128]{0,1:T(8,128)S(1)} %get-tuple-element.21), channel_id=1, source_target_pairs={{0,1},{1,2},{2,3},{3,4},{4,5},{5,6},{6,7},{7,8},{8,9},{9,10},{10,1... | collective-permute-start | bytes 3145736 | tf_op jit(solution)/shard_map/ppermute | solution.py:150
  557.4 17.3 %collective-permute-start.5 = (f32[2048,128]{0,1:T(8,128)S(1)}, f32[2048,128]{0,1:T(8,128)S(1)}, u32[]{:S(2)}, u32[]{:S(2)}) collective-permute-start(f32[2048,128]{0,1:T(8,128)S(1)} %get-tuple-element.22), channel_id=1, source_target_pairs={{1,0},{2,1},{3,2},{4,3},{5,4},{6,5},{7,6},{8,7},{9,8},{10,9},{11,1... | collective-permute-start | bytes 3145736 | tf_op jit(solution)/shard_map/ppermute | solution.py:150
Sparse Core Ops, SparseCore 0:
  86.0 81.7 all-gather.2

commit v2 on v1

--- a/solution.py
+++ b/solution.py
@@ -136,97 +136,558 @@
             pltpu.VMEM((width, 1), F32),
             pltpu.VMEM((width, width), F32),
         ],
+        compiler_params=pltpu.CompilerParams(vmem_limit_bytes=14 * 2**20),
         name="rotation",
     )(gram)
 
 
-def gathered_total(array, axis):
-    return lax.all_gather(array, axis).sum(0)
-
-
-def shifted(block, axis, distance):
-    devices = range(lax.axis_size(axis))
-    route = [(i - distance, i) for i in devices if i - distance in devices]
-    return lax.ppermute(block, axis, route)
-
-
-def sent_to_all(array, axis):
-    devices = lax.axis_size(axis)
-    return lax.all_to_all(
-        jnp.broadcast_to(array[None], (devices, *array.shape)), axis, 0, 0, tiled=True
+MESH = pl.DeviceIdType.MESH
+CHUNK = 256
+GRANT = 14 * 2**20
+
+
+def greet(peers):
+    barrier = pltpu.get_barrier_semaphore()
+    for peer, wanted in peers:
+        if wanted is None:
+            pl.semaphore_signal(barrier, inc=1, device_id=peer, device_id_type=MESH)
+        else:
+
+            @pl.when(wanted)
+            def _(peer=peer):
+                pl.semaphore_signal(barrier, inc=1, device_id=peer, device_id_type=MESH)
+
+
+def met(count):
+    pl.semaphore_wait(pltpu.get_barrier_semaphore(), count)
+
+
+def row_place(grid):
+    deep, wide = grid
+    me = lax.axis_index("row")
+    return me // wide, me % wide
+
+
+def row_peers(grid):
+    deep, wide = grid
+    down, across = row_place(grid)
+    peers = [({"row": down * wide + (across + j) % wide}, None) for j in range(1, wide)]
+    return peers + [({"row": (down + j) % deep * wide + across}, None) for j in range(1, deep)]
+
+
+def row_total(grid, part, total, slots, sums, send, recv):
+    deep, wide = grid
+    down, across = row_place(grid)
+    piece = part.shape[0] // wide
+    mine = pl.ds(pl.multiple_of(across * piece, 8), piece)
+
+    def across_peer(j):
+        return {"row": down * wide + (across + j) % wide}
+
+    scatter = []
+    for j in range(1, wide):
+        theirs = pl.ds(pl.multiple_of((across + j) % wide * piece, 8), piece)
+        scatter.append(
+            pltpu.make_async_remote_copy(
+                part.at[theirs], slots.at[j - 1], send.at[0, j], recv.at[0, j], across_peer(j), MESH
+            )
+        )
+        scatter[-1].start()
+    for copy in scatter:
+        copy.wait_recv()
+    value = part[mine, :]
+    for j in range(1, wide):
+        value = value + slots[j - 1]
+    sums[down] = value
+    exchange = []
+    for j in range(1, deep):
+        peer = {"row": (down + j) % deep * wide + across}
+        exchange.append(
+            pltpu.make_async_remote_copy(
+                sums.at[down], sums.at[down], send.at[1, j], recv.at[1, j], peer, MESH
+            )
+        )
+        exchange[-1].start()
+    for copy in exchange:
+        copy.wait_recv()
+    value = sums[0]
+    for j in range(1, deep):
+        value = value + sums[j]
+    total[mine, :] = value
+    gather = []
+    for j in range(1, wide):
+        gather.append(
+            pltpu.make_async_remote_copy(
+                total.at[mine], total.at[mine], send.at[2, j], recv.at[2, j], across_peer(j), MESH
+            )
+        )
+        gather[-1].start()
+    for copy in gather:
+        copy.wait_recv()
+    for copy in scatter + exchange + gather:
+        copy.wait_send()
+
+
+def total_scratch(grid, rows, block):
+    deep, wide = grid
+    steps = max(grid)
+    return [
+        pltpu.VMEM((rows, block), F32),
+        pltpu.VMEM((rows, block), F32),
+        pltpu.VMEM((wide, rows // wide, block), F32),
+        pltpu.VMEM((deep, rows // wide, block), F32),
+        pltpu.SemaphoreType.DMA((3, steps)),
+        pltpu.SemaphoreType.DMA((3, steps)),
+    ]
+
+
+def turn_and_move(
+    blocks, rotation, fresh, ahead, back, send, recv, spin_high, spin_low, first, last, position, count
+):
+    block = blocks.shape[2]
+    chunks = blocks.shape[1] // CHUNK
+    high, low = halves(rotation[...])
+    spin_high[...] = high
+    spin_low[...] = low
+
+    def copies(c):
+        rows = pl.ds(pl.multiple_of(c * CHUNK, CHUNK), CHUNK)
+        onward = pltpu.make_async_remote_copy(
+            ahead.at[rows], fresh.at[0, rows], send.at[0, c], recv.at[0, c], {"pair": position + 1}, MESH
+        )
+        return rows, onward, pltpu.make_async_remote_copy(
+            back.at[rows], fresh.at[1, rows], send.at[1, c], recv.at[1, c], {"pair": position - 1}, MESH
+        )
+
+    def turn(c, _):
+        rows, _, _ = copies(c)
+        pair = jnp.concatenate([blocks[0, rows, :], blocks[1, rows, :]], axis=1)
+        turned = product(halves(pair), (spin_high[...], spin_low[...]))
+        upper, lower = turned[:, :block], turned[:, block:]
+        ahead[rows, :] = jnp.where(first, lower, upper)
+        back[rows, :] = lower
+
+        @pl.when(first)
+        def _():
+            fresh[0, rows, :] = upper
+
+        @pl.when(last)
+        def _():
+            fresh[1, rows, :] = upper
+
+        return 0
+
+    def leave(c, _):
+        _, onward, backward = copies(c)
+
+        @pl.when(jnp.logical_not(last))
+        def _():
+            onward.start()
+
+        @pl.when(jnp.logical_not(first))
+        def _():
+            backward.start()
+
+        return 0
+
+    def turn_and_leave(c, _):
+        turn(c, 0)
+        return leave(c, 0)
+
+    early = chunks // 2
+    lax.fori_loop(0, early, turn, 0)
+    met(count)
+    lax.fori_loop(0, early, leave, 0)
+    lax.fori_loop(early, chunks, turn_and_leave, 0)
+
+    def arrive(c):
+        _, onward, backward = copies(c)
+
+        @pl.when(jnp.logical_not(first))
+        def _():
+            onward.wait_recv()
+
+        @pl.when(jnp.logical_not(last))
+        def _():
+            backward.wait_recv()
+
+    def finish():
+        def left(c, _):
+            _, onward, backward = copies(c)
+
+            @pl.when(jnp.logical_not(last))
+            def _():
+                onward.wait_send()
+
+            @pl.when(jnp.logical_not(first))
+            def _():
+                backward.wait_send()
+
+            return 0
+
+        lax.fori_loop(0, chunks, left, 0)
+
+    return arrive, finish
+
+
+def pair_place():
+    position = lax.axis_index("pair")
+    first = position == 0
+    last = position == lax.axis_size("pair") - 1
+    count = jnp.where(first, 0, 1) + jnp.where(last, 0, 1)
+    peers = [
+        ({"pair": position + 1}, jnp.logical_not(last)),
+        ({"pair": position - 1}, jnp.logical_not(first)),
+    ]
+    return position, first, last, peers, count
+
+
+def round_kernel(
+    grid, blocks, rotation, upper_gram, lower_gram, fresh, gram,
+    ahead, back, ahead_gram, back_gram, spin_high, spin_low, send, recv, gram_send, gram_recv,
+    part, total, slots, sums, sum_send, sum_recv,
+):
+    position, first, last, peers, count = pair_place()
+    block = blocks.shape[2]
+    across = row_peers(grid)
+    greet(peers + across)
+    ahead_gram[...] = jnp.where(first, lower_gram[...], upper_gram[...])
+    back_gram[...] = lower_gram[...]
+
+    @pl.when(first)
+    def _():
+        gram[:block, :block] = upper_gram[...]
+
+    @pl.when(last)
+    def _():
+        gram[block:, block:] = upper_gram[...]
+
+    arrive, finish = turn_and_move(
+        blocks, rotation, fresh, ahead, back, send, recv, spin_high, spin_low, first, last, position,
+        count + len(across),
     )
-
-
-def taken_together(array, axis):
-    return sent_to_all(array, axis).sum(axis=0)
-
-
-def inner_rows(left_side, right_side):
-    return lax.dot_general(
-        left_side,
-        right_side,
-        (((0,), (0,)), ((), ())),
-        precision=lax.Precision.HIGHEST,
-        preferred_element_type=jnp.float32,
+    onward = pltpu.make_async_remote_copy(
+        ahead_gram, gram.at[pl.ds(0, block), pl.ds(0, block)], gram_send.at[0], gram_recv.at[0],
+        {"pair": position + 1}, MESH,
     )
-
-
-def full_gram(upper_block, lower_block):
-    pair_cols = jnp.concatenate([upper_block, lower_block], axis=1)
-    return gathered_total(inner_rows(pair_cols, pair_cols), "row")
-
-
-def move_blocks(upper_load, lower_load, position, last_index):
-    sent_on = jnp.where(position == 0, lower_load, upper_load)
-    came_on = shifted(sent_on, "pair", 1)
-    came_back = shifted(lower_load, "pair", -1)
-    new_upper = jnp.where(position == 0, upper_load, came_on)
-    new_lower = jnp.where(position == last_index, upper_load, came_back)
-    return (new_upper, new_lower)
-
-
-def body(embedding, pairing):
+    backward = pltpu.make_async_remote_copy(
+        back_gram, gram.at[pl.ds(block, block), pl.ds(block, block)], gram_send.at[1], gram_recv.at[1],
+        {"pair": position - 1}, MESH,
+    )
+
+    @pl.when(jnp.logical_not(last))
+    def _():
+        onward.start()
+
+    @pl.when(jnp.logical_not(first))
+    def _():
+        backward.start()
+
+    part[...] = jnp.zeros_like(part)
+
+    def cross(c, _):
+        arrive(c)
+        rows = pl.ds(pl.multiple_of(c * CHUNK, CHUNK), CHUNK)
+        part[...] += product(halves(fresh[0, rows, :]), halves(fresh[1, rows, :]), ((0,), (0,)))
+        return 0
+
+    lax.fori_loop(0, blocks.shape[1] // CHUNK, cross, 0)
+    row_total(grid, part, total, slots, sums, sum_send, sum_recv)
+    gram[:block, block:] = total[...]
+    gram[block:, :block] = total[...].T
+
+    @pl.when(jnp.logical_not(first))
+    def _():
+        onward.wait_recv()
+        backward.wait_send()
+
+    @pl.when(jnp.logical_not(last))
+    def _():
+        backward.wait_recv()
+        onward.wait_send()
+
+    finish()
+
+
+def last_kernel(blocks, rotation, fresh, ahead, back, spin_high, spin_low, send, recv):
+    position, first, last, peers, count = pair_place()
+    greet(peers)
+    arrive, finish = turn_and_move(
+        blocks, rotation, fresh, ahead, back, send, recv, spin_high, spin_low, first, last, position, count
+    )
+
+    def take(c, _):
+        arrive(c)
+        return 0
+
+    lax.fori_loop(0, blocks.shape[1] // CHUNK, take, 0)
+    finish()
+
+
+def move_scratch(rows, block):
+    width = 2 * block
+    chunks = rows // CHUNK
+    return (
+        [pltpu.VMEM((rows, block), F32), pltpu.VMEM((rows, block), F32)],
+        [pltpu.VMEM((width, width), BF16), pltpu.VMEM((width, width), BF16)],
+        [pltpu.SemaphoreType.DMA((2, chunks)), pltpu.SemaphoreType.DMA((2, chunks))],
+    )
+
+
+VMEM = pl.BlockSpec(memory_space=pltpu.VMEM)
+
+
+def next_round(blocks, rotation, upper_gram, lower_gram, grid):
+    _, rows, block = blocks.shape
+    loads, spins, sems = move_scratch(rows, block)
+    return pl.pallas_call(
+        functools.partial(round_kernel, grid),
+        out_shape=(
+            jax.ShapeDtypeStruct(blocks.shape, F32),
+            jax.ShapeDtypeStruct((2 * block, 2 * block), F32),
+        ),
+        in_specs=[VMEM] * 4,
+        out_specs=(VMEM, VMEM),
+        scratch_shapes=loads
+        + [pltpu.VMEM((block, block), F32), pltpu.VMEM((block, block), F32)]
+        + spins
+        + sems
+        + [pltpu.SemaphoreType.DMA((2,)), pltpu.SemaphoreType.DMA((2,))]
+        + total_scratch(grid, block, block),
+        compiler_params=pltpu.CompilerParams(collective_id=1, has_side_effects=True, vmem_limit_bytes=GRANT),
+        name="next_round",
+    )(blocks, rotation, upper_gram, lower_gram)
+
+
+def last_round(blocks, rotation):
+    _, rows, block = blocks.shape
+    loads, spins, sems = move_scratch(rows, block)
+    return pl.pallas_call(
+        last_kernel,
+        out_shape=jax.ShapeDtypeStruct(blocks.shape, F32),
+        in_specs=[VMEM] * 2,
+        out_specs=VMEM,
+        scratch_shapes=loads + spins + sems,
+        compiler_params=pltpu.CompilerParams(collective_id=2, has_side_effects=True, vmem_limit_bytes=GRANT),
+        name="last_round",
+    )(blocks, rotation)
+
+
+def pick_kernel(embedding, pairing, picked, sems):
+    slots = pairing.shape[0]
+    block = picked.shape[3]
+
+    def copy(slot):
+        source = pl.ds(pl.multiple_of(pairing[slot] * block, block), block)
+        return pltpu.make_async_copy(embedding.at[:, source], picked.at[slot // 2, slot % 2], sems.at[slot])
+
+    def start(slot, _):
+        copy(slot).start()
+        return 0
+
+    def wait(slot, _):
+        copy(slot).wait()
+        return 0
+
+    lax.fori_loop(0, slots, start, 0)
+    lax.fori_loop(0, slots, wait, 0)
+
+
+def pick(embedding, pairing):
     sub_rows, columns = embedding.shape
     slots = pairing.shape[0]
-    block = columns // slots
-    ordered = jnp.take(embedding.reshape(sub_rows, slots, block), pairing, axis=1).reshape(
-        sub_rows, columns
-    )
-    local = lax.all_to_all(ordered, "pair", split_axis=1, concat_axis=0, tiled=True)
-    rows_here = local.shape[0]
-    total_rows = rows_here * lax.axis_size("row")
-    position = lax.axis_index("pair")
-    last_index = lax.axis_size("pair") - 1
-    upper_block = local[:, :block]
-    lower_block = local[:, block:]
-    gram_mat = full_gram(upper_block, lower_block)
+    return pl.pallas_call(
+        pick_kernel,
+        out_shape=jax.ShapeDtypeStruct((slots // 2, 2, sub_rows, columns // slots), F32),
+        in_specs=[pl.BlockSpec(memory_space=pl.ANY), pl.BlockSpec(memory_space=pltpu.SMEM)],
+        out_specs=VMEM,
+        scratch_shapes=[pltpu.SemaphoreType.DMA((slots,))],
+        compiler_params=pltpu.CompilerParams(vmem_limit_bytes=GRANT),
+        name="pick",
+    )(embedding, pairing)
+
+
+def deal_kernel(
+    grid, cut, outgoing, blocks, gram, relayed, send, recv, relay_send, relay_recv, own,
+    part, total, slots, sums, sum_send, sum_recv,
+):
+    tall, ring, cores = cut
+    sub_rows = outgoing.shape[2]
+    block = blocks.shape[2]
+    devices = lax.axis_size("pair")
+    me = lax.axis_index("pair")
+    core, turn, side = me % cores, me // cores % ring, me // (cores * ring)
+    halfway = ring // 2
+    group = tall * cores
+
+    def device(there_side, there_turn, there_core):
+        return (there_side % tall * ring + (there_turn + 2 * ring) % ring) * cores + there_core % cores
+
+    def target_of(far, near):
+        return device(side + near // cores, turn + far, core + near % cores)
+
+    def rows_of(index):
+        return pl.ds(pl.multiple_of(index * sub_rows, sub_rows), sub_rows)
+
+    def far_of(order):
+        away = (order + 1) // 2
+        return halfway + away - 2 * away * (order % 2)
+
+    def copy_at(far, near):
+        target = target_of(far, near)
+        step = far * group + near
+        return pltpu.make_async_remote_copy(
+            outgoing.at[target], blocks.at[:, rows_of(me), :], send.at[step], recv.at[step], {"pair": target}, MESH
+        )
+
+    def relay_at(over):
+        near = over * cores + 1
+        target = target_of(halfway, near)
+        between = device(side + over, turn - halfway // 2, core + 1)
+        step = halfway * group + near
+        return pltpu.make_async_remote_copy(
+            outgoing.at[target], relayed.at[over], send.at[step], relay_recv.at[over], {"pair": between}, MESH
+        )
+
+    def forward_at(over):
+        step = halfway * group + over * cores + 1
+        origin = device(side - over + tall, turn + halfway // 2, core + 1)
+        return pltpu.make_async_remote_copy(
+            relayed.at[over], blocks.at[:, rows_of(origin), :], relay_send.at[over], recv.at[step],
+            {"pair": device(side, turn - halfway // 2, core)}, MESH,
+        )
+
+    barrier = pltpu.get_barrier_semaphore()
+
+    def call(step, _):
+        target = target_of(step // group, step % group)
+        pl.semaphore_signal(barrier, inc=1, device_id={"pair": target}, device_id_type=MESH)
+        return 0
+
+    lax.fori_loop(1, devices, call, 0)
+    across = row_peers(grid)
+    greet(across)
+    keep = pltpu.make_async_copy(outgoing.at[me], blocks.at[:, rows_of(me), :], own)
+    keep.start()
+    met(devices - 1 + len(across))
+    for over in range(tall):
+        relay_at(over).start()
+        for there in range(0, cores, 2):
+            copy_at(halfway, over * cores + there).start()
+
+    def send_all(order, _):
+        for near in range(group):
+            copy_at(far_of(order), near).start()
+        return 0
+
+    lax.fori_loop(1, ring - 1, send_all, 0)
+    for near in range(1, group):
+        copy_at(0, near).start()
+    for over in range(tall):
+        relay_at(over).wait_recv()
+        forward_at(over).start()
+    keep.wait()
+    part[...] = jnp.zeros_like(part)
+
+    def add(order, _):
+        far = far_of(order)
+        for near in range(group):
+
+            @pl.when(far * group + near > 0)
+            def _(near=near):
+                copy_at(far, near).wait_recv()
+
+        for there in range(tall):
+            source = (there * ring + (turn - far + ring) % ring) * cores
+            rows = pl.ds(pl.multiple_of(source * sub_rows, sub_rows * cores), sub_rows * cores)
+            high, low = halves(jnp.concatenate([blocks[0, rows, :], blocks[1, rows, :]], axis=1))
+
+            def one(x, y):
+                return lax.dot_general(x, y, (((0,), (0,)), ((), ())), preferred_element_type=F32)
+
+            main, side_part = one(high, high), one(high, low)
+            whole = main + (side_part + side_part.T)
+            part[:block, :] += whole[:block, :block]
+            part[block : 2 * block, :] += whole[:block, block:]
+            part[2 * block :, :] += whole[block:, block:]
+        return 0
+
+    lax.fori_loop(0, ring, add, 0)
+    row_total(grid, part, total, slots, sums, sum_send, sum_recv)
+    gram[:block, :block] = total[:block, :]
+    gram[:block, block:] = total[block : 2 * block, :]
+    gram[block:, :block] = total[block : 2 * block, :].T
+    gram[block:, block:] = total[2 * block :, :]
+
+    def sent(step, _):
+        copy_at(step // group, step % group).wait_send()
+        return 0
+
+    lax.fori_loop(1, devices, sent, 0)
+    for over in range(tall):
+        forward_at(over).wait_send()
+
+
+def deal(picked, grid, cut):
+    devices, _, sub_rows, block = picked.shape
+    return pl.pallas_call(
+        functools.partial(deal_kernel, grid, cut),
+        out_shape=(
+            jax.ShapeDtypeStruct((2, sub_rows * devices, block), F32),
+            jax.ShapeDtypeStruct((2 * block, 2 * block), F32),
+        ),
+        in_specs=[VMEM],
+        out_specs=(VMEM, VMEM),
+        scratch_shapes=[
+            pltpu.VMEM((cut[0], 2, sub_rows, block), F32),
+            pltpu.SemaphoreType.DMA((devices,)),
+            pltpu.SemaphoreType.DMA((devices,)),
+            pltpu.SemaphoreType.DMA((cut[0],)),
+            pltpu.SemaphoreType.DMA((cut[0],)),
+            pltpu.SemaphoreType.DMA,
+        ]
+        + total_scratch(grid, 3 * block, block),
+        compiler_params=pltpu.CompilerParams(collective_id=0, has_side_effects=True, vmem_limit_bytes=GRANT),
+        name="deal",
+    )(picked)
+
+
+def join_kernel(blocks, joined):
+    block = blocks.shape[2]
+    joined[:, :block] = blocks[0]
+    joined[:, block:] = blocks[1]
+
+
+def join(blocks):
+    _, rows, block = blocks.shape
+    return pl.pallas_call(
+        join_kernel,
+        grid=(rows // CHUNK,),
+        out_shape=jax.ShapeDtypeStruct((rows, 2 * block), F32),
+        in_specs=[pl.BlockSpec((2, CHUNK, block), lambda i: (0, i, 0))],
+        out_specs=pl.BlockSpec((CHUNK, 2 * block), lambda i: (i, 0)),
+        compiler_params=pltpu.CompilerParams(vmem_limit_bytes=GRANT),
+        name="join",
+    )(blocks)
+
+
+def cuts():
+    grids = {16: (4, 4), 4: (2, 2)}
+    pairs = {32: (2, 8, 2), 4: (1, 2, 2)}
+    return grids[lax.axis_size("row")], pairs[lax.axis_size("pair")]
+
+
+def body(embedding, pairing):
+    grid, cut = cuts()
+    blocks, gram = deal(pick(embedding, pairing), grid, cut)
+    total_rows = blocks.shape[1] * lax.axis_size("row")
     for round_num in range(ROUNDS):
-        rotation, upper_gram, lower_gram = make_rotation(gram_mat, total_rows)
-        pair_cols = jnp.concatenate([upper_block, lower_block], axis=1)
-        turned = jnp.dot(
-            pair_cols, rotation, precision=lax.Precision.HIGHEST, preferred_element_type=jnp.float32
-        )
-        upper_block = turned[:, :block]
-        lower_block = turned[:, block:]
+        rotation, upper_gram, lower_gram = make_rotation(gram, total_rows)
         if round_num + 1 < ROUNDS:
-            upper_load = jnp.concatenate([upper_block, upper_gram], axis=0)
-            lower_load = jnp.concatenate([lower_block, lower_gram], axis=0)
-            upper_load, lower_load = move_blocks(upper_load, lower_load, position, last_index)
-            upper_block = upper_load[:rows_here]
-            upper_gram = upper_load[rows_here:]
-            lower_block = lower_load[:rows_here]
-            lower_gram = lower_load[rows_here:]
-            cross = taken_together(inner_rows(upper_block, lower_block), "row")
-            gram_mat = jnp.concatenate(
-                [
-                    jnp.concatenate([upper_gram, cross], axis=1),
-                    jnp.concatenate([cross.T, lower_gram], axis=1),
-                ],
-                axis=0,
-            )
+            blocks, gram = next_round(blocks, rotation, upper_gram, lower_gram, grid)
         else:
-            upper_block, lower_block = move_blocks(upper_block, lower_block, position, last_index)
-    return jnp.concatenate([upper_block, lower_block], axis=1)
+            blocks = last_round(blocks, rotation)
+    return join(blocks)
 
 
 def solution(mesh):

time: 590 us -> 404 us (0.68)
  the two profiles are of different devices: /device:TPU:207 before, /device:TPU:393 now
where the time goes in v2:
time: 404 us; the launch traced here: 397 us
  Pallas kernels  394 us (98%)
    pallas_call x3, Pallas kernels, make_rotation(): pl.pallas_call(functools.partial(rotation_kernel, total_rows), out_shape=...  173 us
    pallas_call x1, Pallas kernels, last_round(): pl.pallas_call(last_kernel, out_shape=jax.ShapeDtypeStruct(blocks.shape,...  77.5 us
    pallas_call x1, Pallas kernels, deal(): pl.pallas_call(functools.partial(deal_kernel, grid, cut), out_shape=(jax....  75.8 us
    pallas_call x2, Pallas kernels, next_round(): pl.pallas_call(functools.partial(round_kernel, grid), out_shape=(jax.Shap...  62.1 us

profile of v2, /device:TPU:393, one launch (start us, length us, event | category | flops | bytes accessed | tf_op | source)
XLA Modules:
  0.0 396.6 jit_solution(16622472917226112585)
XLA Ops:
  0.0 0.0 copy-start
  0.0 1.6 copy-done
  1.6 0.0 copy-start.1
  1.6 0.7 copy-done.1
  2.2 2.8 pick.1.outgoing
  5.0 75.8 %deal.1 = (f32[2,2048,128]{2,1,0:T(8,128)S(1)}, f32[256,256]{1,0:T(8,128)S(1)}) custom-call(f32[32,2,64,128]{3,2,1,0:T(8,128)S(1)} %pick.1.outgoing), custom_call_target="tpu_custom_call" | custom-call | tf_op jit(solution)/shard_map/deal/pallas_call | solution.py:633
  80.9 82.2 %rotation.3 = (f32[256,256]{1,0:T(8,128)S(1)}, f32[128,128]{1,0:T(8,128)S(1)}, f32[128,128]{1,0:T(8,128)S(1)}) custom-call(f32[256,256]{1,0:T(8,128)S(1)} %get-tuple-element.19.gram_ref), custom_call_target="tpu_custom_call" | custom-call | tf_op jit(solution)/shard_map/rotation/pallas_call | solution.py:124
  163.0 34.9 %next_round.2 = (f32[2,2048,128]{2,1,0:T(8,128)S(1)}, f32[256,256]{1,0:T(8,128)S(1)}) custom-call(f32[2,2048,128]{2,1,0:T(8,128)S(1)} %get-tuple-element.18.blocks, f32[256,256]{1,0:T(8,128)S(1)} %get-tuple-element.20.rotation, f32[128,128]{1,0:T(8,128)S(1)} %get-tuple-element.21.upper_gram, f32[128,128]{1,0:T(8,128)S(1)} %get-tuple-element.22.lower_gram), custom_call_target="tpu_custom_call" | custom-call | tf_op jit(solution)/shard_map/next_round/pallas_call | solution.py:443
  198.0 82.1 %rotation.4 = (f32[256,256]{1,0:T(8,128)S(1)}, f32[128,128]{1,0:T(8,128)S(1)}, f32[128,128]{1,0:T(8,128)S(1)}) custom-call(f32[256,256]{1,0:T(8,128)S(1)} %get-tuple-element.24.gram_ref), custom_call_target="tpu_custom_call" | custom-call | tf_op jit(solution)/shard_map/rotation/pallas_call | solution.py:124
  280.1 27.1 %next_round.3 = (f32[2,2048,128]{2,1,0:T(8,128)S(1)}, f32[256,256]{1,0:T(8,128)S(1)}) custom-call(f32[2,2048,128]{2,1,0:T(8,128)S(1)} %get-tuple-element.23.blocks, f32[256,256]{1,0:T(8,128)S(1)} %get-tuple-element.25.rotation, f32[128,128]{1,0:T(8,128)S(1)} %get-tuple-element.26.upper_gram, f32[128,128]{1,0:T(8,128)S(1)} %get-tuple-element.27.lower_gram), custom_call_target="tpu_custom_call" | custom-call | tf_op jit(solution)/shard_map/next_round/pallas_call | solution.py:443
  307.3 8.8 %rotation.5 = (f32[256,256]{1,0:T(8,128)S(1)}, f32[128,128]{1,0:T(8,128)}, f32[128,128]{1,0:T(8,128)}) custom-call(f32[256,256]{1,0:T(8,128)S(1)} %get-tuple-element.29.gram_ref), custom_call_target="tpu_custom_call" | custom-call | tf_op jit(solution)/shard_map/rotation/pallas_call | solution.py:124
  316.1 77.5 %last_round.1.blocks = f32[2,2048,128]{2,1,0:T(8,128)S(1)} custom-call(f32[2,2048,128]{2,1,0:T(8,128)S(1)} %get-tuple-element.28.blocks, f32[256,256]{1,0:T(8,128)S(1)} %get-tuple-element.30.rotation), custom_call_target="tpu_custom_call" | custom-call | tf_op jit(solution)/shard_map/last_round/pallas_call | solution.py:465
  393.6 3.1 join.1
Async XLA Ops:
  0.0 1.6 copy-start
  1.6 0.7 copy-start.1
